TPU v7x, 128 devices: a whole 4x4x4 slice. The times are simulated.
128 devices in a mesh: wide: 32 (over x, z, core), narrow: 4 (over y).
Axes of the slice: x: 4, y: 4, z: 4, core: 2. Of those that a mesh axis runs over, the one named last changes fastest.
Arguments:
- front: bfloat16 [4, 32, 128, 32, 4, 128], P(None, 'wide', None, None, 'narrow'), may hold values from -6 to 6
- pivot_inverse: bfloat16 [4, 128, 128], replicated, may hold values from -0.0105112052 to 0.17838107
- rhs: bfloat16 [4, 32, 128, 256], P(None, 'wide'), may hold values from -6 to 6
- trail_sol: bfloat16 [4, 32, 128, 256], P(None, 'wide'), may hold values from -1.1953125 to 1.1953125
- block_mask: int32 [4, 32, 32, 4], P(None, 'wide', None, 'narrow'), may hold values 0 or 1
- panel_order: int32 [4], replicated, may hold values from 0 to 3, each once
Outputs:
- front_out: bfloat16 [4, 32, 128, 32, 4, 128], P(None, 'wide', None, None, 'narrow')
- forward_rhs: bfloat16 [4, 32, 128, 256], P(None, 'wide')
- window_solution: bfloat16 [4, 128, 256], replicated
Inputs may be any that keep to these rules, and one draw needn't show every extreme that they name: `panel_order`: each value 0 to 3 appears once.
All inputs are finite; a program needn't handle non-finite values. No bound on the sum of `block_mask` on one device may be relied on, other than what follows from the above.
Results may differ from a plain program's by a relative error of at most 0.0076.
Values may be sent and summed in bfloat16 or wider, within the bound.
No kernel may reach another device: no remote copies, remote signals or barrier semaphores. Data moves between devices by JAX's collectives and lax.ppermute only.
A program may use at most 64 MiB of HBM per device.

v0:
```python
import jax
import jax.numpy as jnp
from jax import lax
from jax.sharding import PartitionSpec as P


def spread(block, axis, source):
    block = jnp.where(lax.axis_index(axis) == source, block, jnp.zeros_like(block))
    return lax.psum(block, axis)


def body(front, pivot_inverse, rhs, trail_sol, block_mask, panel_order):
    rloc = front.shape[0]
    bsize = front.shape[2]
    cloc = front.shape[3]
    nrhs_local = rhs.shape[3]
    panels = panel_order.shape[0]
    nwide = lax.axis_size("wide")
    nnarrow = lax.axis_size("narrow")
    blocks = front.reshape(rloc, bsize, cloc, bsize)
    pattern = block_mask.reshape(rloc, cloc).astype(jnp.float32)
    right = rhs.reshape(rloc, bsize, nrhs_local)
    rows_global = jnp.arange(rloc, dtype=jnp.int32) * nwide + lax.axis_index("wide")
    cols_global = jnp.arange(cloc, dtype=jnp.int32) * nnarrow + lax.axis_index("narrow")
    section_ids = jnp.arange(panels, dtype=jnp.int32)
    rows_rank = jnp.min(
        jnp.where(rows_global[:, None] == panel_order[None, :], section_ids[None, :], panels),
        axis=1,
    )
    cols_rank = jnp.min(
        jnp.where(cols_global[:, None] == panel_order[None, :], section_ids[None, :], panels),
        axis=1,
    )

    def pivot_weight(target):
        return lax.dynamic_index_in_dim(pivot_inverse, target, 0, keepdims=False)

    def panel_factors(col_blocks, row_blocks, target, section):
        weight = pivot_weight(target)
        left = jnp.einsum("rab,bc->rac", col_blocks, weight, preferred_element_type=jnp.float32)
        left = jnp.where((rows_rank > section)[:, None, None], left, 0.0).astype(jnp.bfloat16)
        left = spread(left, "narrow", target % nnarrow)
        upper = jnp.einsum("ac,ajb->cjb", weight, row_blocks, preferred_element_type=jnp.float32)
        upper = jnp.where((cols_rank > section)[None, :, None], upper, 0.0).astype(jnp.bfloat16)
        upper = spread(upper, "wide", target % nwide)
        return (left, upper)

    def column_of(current, target):
        return lax.dynamic_index_in_dim(current, target // nnarrow, 2, keepdims=False)

    def row_of(current, target):
        return lax.dynamic_index_in_dim(current, target // nwide, 0, keepdims=False)

    saved_left = []
    saved_pivot = []
    left, upper = panel_factors(
        column_of(blocks, panel_order[0]), row_of(blocks, panel_order[0]), panel_order[0], 0
    )
    for section in range(panels):
        target = panel_order[section]
        weight = pivot_weight(target)
        product = jnp.einsum("rac,cjb->rajb", left, upper, preferred_element_type=jnp.float32)
        blocks = (blocks.astype(jnp.float32) - pattern[:, None, :, None] * product).astype(
            jnp.bfloat16
        )
        if section + 1 < panels:
            following = panel_order[section + 1]
            next_left, next_upper = panel_factors(
                column_of(blocks, following), row_of(blocks, following), following, section + 1
            )
        pivot_rhs = lax.dynamic_index_in_dim(right, target // nwide, 0, keepdims=False)
        solved = jnp.einsum(
            "ac,an->cn", weight, pivot_rhs, preferred_element_type=jnp.float32
        ).astype(jnp.bfloat16)
        solved = spread(solved, "wide", target % nwide)
        elimination = jnp.einsum("rac,cn->ran", left, solved, preferred_element_type=jnp.float32)
        right = (right.astype(jnp.float32) - elimination).astype(jnp.bfloat16)
        saved_left.append(left)
        saved_pivot.append(solved)
        if section + 1 < panels:
            left, upper = (next_left, next_upper)
    current = trail_sol.reshape(rloc, bsize, nrhs_local)
    window = jnp.zeros((panels, bsize, nrhs_local), jnp.bfloat16)
    for section in reversed(range(panels)):
        target = panel_order[section]
        partial_sum = jnp.einsum(
            "rac,ran->cn", saved_left[section], current, preferred_element_type=jnp.float32
        )
        total = lax.psum(partial_sum, "wide")
        corrected = (saved_pivot[section].astype(jnp.float32) - total).astype(jnp.bfloat16)
        result = jnp.einsum(
            "ac,cn->an", pivot_weight(target), corrected, preferred_element_type=jnp.float32
        ).astype(jnp.bfloat16)
        current = jnp.where((rows_global == target)[:, None, None], result[None], current)
        window = lax.dynamic_update_index_in_dim(window, result, target, 0)
    return (blocks.reshape(front.shape), right.reshape(rhs.shape), window)


def solution(mesh):
    in_specs = (
        P(None, "wide", None, None, "narrow", None),
        P(),
        P(None, "wide", None, None),
        P(None, "wide", None, None),
        P(None, "wide", None, "narrow"),
        P(),
    )
    out_specs = (P(None, "wide", None, None, "narrow", None), P(None, "wide", None, None), P())
    return jax.shard_map(body, mesh=mesh, in_specs=in_specs, out_specs=out_specs, check_vma=False)
```

profile of v0, /device:TPU:1, one launch (start us, length us, event | category | flops | bytes accessed | tf_op | source)
XLA Modules:
  0.0 1070.7 jit_solution(9461470469571352421)
XLA Ops:
  7.2 1.5 fusion.111
  12.6 0.8 select_reduce_fusion.1
  13.5 1.5 constant_dynamic-slice_fusion.1
  15.0 0.8 fusion.18
  16.0 1.3 constant_dynamic-slice_fusion
  17.3 0.7 select_reduce_fusion
  18.1 1.6 fusion.2
  19.7 0.8 fusion.19
  24.1 34.5 %all-reduce.17.cloned.1.call-done = bf16[4,128,128]{2,1,0:T(8,128)(2,1)} async-done(((bf16[4,128,128]{2,1,0:T(8,128)(2,1)}), bf16[4,128,128]{2,1,0:T(8,128)(2,1)}) %all-reduce.17.cloned.1.call-update) | async-done | bytes 131088 | tf_op jit(solution)/shard_map/psum | solution.py:9
  58.6 112.0 %all-reduce.39.cloned.1.call-done = (bf16[128,32,128]{2,0,1:T(8,128)(2,1)}, bf16[128,256]{1,0:T(8,128)(2,1)}) async-done(((bf16[128,32,128]{2,0,1:T(8,128)(2,1)}, bf16[128,256]{1,0:T(8,128)(2,1)}), (bf16[128,32,128]{2,0,1:T(8,128)(2,1)}, bf16[128,256]{1,0:T(8,128)(2,1)})) %all-reduce.39.cloned.1.call-update) | async-done | bytes 1114128 | tf_op jit(solution)/shard_map/psum | solution.py:9
  170.6 4.7 fusion
  175.3 2.0 copy-done.2
  177.3 0.8 fusion.17
  178.2 2.7 fusion.3
  181.1 0.8 fusion.20
  185.6 31.7 %all-reduce.19.cloned.1.call-done = bf16[4,128,128]{2,1,0:T(8,128)(2,1)} async-done(((bf16[4,128,128]{2,1,0:T(8,128)(2,1)}), bf16[4,128,128]{2,1,0:T(8,128)(2,1)}) %all-reduce.19.cloned.1.call-update) | async-done | bytes 131088 | tf_op jit(solution)/shard_map/psum | solution.py:9
  217.3 111.8 %all-reduce.37.cloned.1.call-done = (bf16[128,32,128]{2,0,1:T(8,128)(2,1)}, bf16[128,256]{1,0:T(8,128)(2,1)}) async-done(((bf16[128,32,128]{2,0,1:T(8,128)(2,1)}, bf16[128,256]{1,0:T(8,128)(2,1)}), (bf16[128,32,128]{2,0,1:T(8,128)(2,1)}, bf16[128,256]{1,0:T(8,128)(2,1)})) %all-reduce.37.cloned.1.call-update) | async-done | bytes 1114128 | tf_op jit(solution)/shard_map/psum | solution.py:9
  329.1 3.8 subtract_convert_fusion.2
  333.0 2.0 copy-done.1
  335.0 0.8 fusion.16
  335.9 2.7 fusion.4
  338.8 0.8 fusion.21
  343.9 31.0 %all-reduce.21.cloned.1.call-done = bf16[4,128,128]{2,1,0:T(8,128)(2,1)} async-done(((bf16[4,128,128]{2,1,0:T(8,128)(2,1)}), bf16[4,128,128]{2,1,0:T(8,128)(2,1)}) %all-reduce.21.cloned.1.call-update) | async-done | bytes 131088 | tf_op jit(solution)/shard_map/psum | solution.py:9
  374.9 111.8 %all-reduce.35.cloned.1.call-done = (bf16[128,32,128]{2,0,1:T(8,128)(2,1)}, bf16[128,256]{1,0:T(8,128)(2,1)}) async-done(((bf16[128,32,128]{2,0,1:T(8,128)(2,1)}, bf16[128,256]{1,0:T(8,128)(2,1)}), (bf16[128,32,128]{2,0,1:T(8,128)(2,1)}, bf16[128,256]{1,0:T(8,128)(2,1)})) %all-reduce.35.cloned.1.call-update) | async-done | bytes 1114128 | tf_op jit(solution)/shard_map/psum | solution.py:9
  486.7 3.8 subtract_convert_fusion.1
  490.6 2.0 copy-done.3
  492.6 0.8 fusion.15
  493.5 2.7 fusion.5
  496.4 36.1 %all-reduce.23.cloned.1.call-done = bf16[4,128,128]{2,1,0:T(8,128)(2,1)} async-done(((bf16[4,128,128]{2,1,0:T(8,128)(2,1)}), bf16[4,128,128]{2,1,0:T(8,128)(2,1)}) %all-reduce.23.cloned.1.call-update) | async-done | bytes 131088 | tf_op jit(solution)/shard_map/psum | solution.py:9
  532.5 1.9 convolution_bitcast_fusion.3
  534.5 0.8 fusion.22
  535.4 0.7 broadcast_compare_fusion.2
  536.7 103.3 %all-reduce.25.cloned.1.call-done = f32[128,256]{1,0:T(8,128)} async-done(((f32[128,256]{1,0:T(8,128)}), f32[128,256]{1,0:T(8,128)}) %all-reduce.25.cloned.1.call-update) | async-done | bytes 131088 | tf_op jit(solution)/shard_map/psum | solution.py:89
  639.9 109.0 %all-reduce.33.cloned.1.call-done = (bf16[128,32,128]{2,0,1:T(8,128)(2,1)}, bf16[128,256]{1,0:T(8,128)(2,1)}) async-done(((bf16[128,32,128]{2,0,1:T(8,128)(2,1)}, bf16[128,256]{1,0:T(8,128)(2,1)}), (bf16[128,32,128]{2,0,1:T(8,128)(2,1)}, bf16[128,256]{1,0:T(8,128)(2,1)})) %all-reduce.33.cloned.1.call-update) | async-done | bytes 1114128 | tf_op jit(solution)/shard_map/psum | solution.py:9
  749.0 1.1 bitcast_dynamic-update-slice_fusion.2
  750.0 0.9 convolution_bitcast_fusion.2
  751.6 101.7 %all-reduce.27.cloned.1.call-done = f32[128,256]{1,0:T(8,128)} async-done(((f32[128,256]{1,0:T(8,128)}), f32[128,256]{1,0:T(8,128)}) %all-reduce.27.cloned.1.call-update) | async-done | bytes 131088 | tf_op jit(solution)/shard_map/psum | solution.py:89
  853.3 1.1 bitcast_dynamic-update-slice_fusion.1
  854.3 0.9 convolution_bitcast_fusion.1
  855.5 5.7 fusion.1
  861.3 96.5 %all-reduce.29.cloned.1.call-done = f32[128,256]{1,0:T(8,128)} async-done(((f32[128,256]{1,0:T(8,128)}), f32[128,256]{1,0:T(8,128)}) %all-reduce.29.cloned.1.call-update) | async-done | bytes 131088 | tf_op jit(solution)/shard_map/psum | solution.py:89
  957.7 1.1 bitcast_dynamic-update-slice_fusion
  958.8 0.9 convolution_bitcast_fusion
  959.8 0.9 fusion.10
  960.7 6.9 copy.30
  967.6 94.5 %all-reduce.31.cloned.1.call-done = f32[128,256]{1,0:T(8,128)} async-done(((f32[128,256]{1,0:T(8,128)}), f32[128,256]{1,0:T(8,128)}) %all-reduce.31.cloned.1.call-update) | async-done | bytes 131088 | tf_op jit(solution)/shard_map/psum | solution.py:89
  1062.1 1.0 fusion.24
  1063.1 0.7 copy-done.10
  (63 shorter events, 2.8 us)
Async XLA Ops:
  7.2 7.9 copy-start
  7.2 12.5 %copy-start.9 = (bf16[4,1,128,256]{3,2,1,0:T(8,128)(2,1)S(1)}, bf16[4,1,128,256]{3,2,1,0:T(8,128)(2,1)}, u32[]{:S(2)}) copy-start(bf16[4,1,128,256]{3,2,1,0:T(8,128)(2,1)} %param.8) | copy-start | bytes 786436
  7.2 16.3 %copy-start.15 = (s32[4,1,32,1]{2,3,1,0:T(1,128)S(1)}, s32[4,1,32,1]{2,3,1,0:T(1,128)}, u32[]{:S(2)}) copy-start(s32[4,1,32,1]{2,3,1,0:T(1,128)} %param.10) | copy-start | bytes 1540
  7.2 51.4 %all-reduce.17.cloned.1.call-start = ((), (), s32[]{:S(2)}) async-start(), calls=%async_computation | async-start | bytes 262144 | tf_op jit(solution)/shard_map/psum | solution.py:9
  15.9 154.7 %all-reduce.39.cloned.1.call-start = ((), (), s32[]{:S(2)}) async-start(), calls=%async_computation.11 | async-start | bytes 2228224 | tf_op jit(solution)/shard_map/psum | solution.py:9
  20.5 196.7 %all-reduce.19.cloned.1.call-start = ((), (), s32[]{:S(2)}) async-start(), calls=%async_computation.1 | async-start | bytes 262144 | tf_op jit(solution)/shard_map/psum | solution.py:9
  170.6 10.3 copy-start.7
  170.6 10.3 copy-start.11
  175.3 2.0 copy-start.2
  178.2 150.9 %all-reduce.37.cloned.1.call-start = ((), (), s32[]{:S(2)}) async-start(), calls=%async_computation.10 | async-start | bytes 2228224 | tf_op jit(solution)/shard_map/psum | solution.py:9
  182.0 192.9 %all-reduce.21.cloned.1.call-start = ((), (), s32[]{:S(2)}) async-start(), calls=%async_computation.2 | async-start | bytes 262144 | tf_op jit(solution)/shard_map/psum | solution.py:9
  329.1 9.5 copy-start.8
  329.1 9.5 copy-start.12
  333.0 2.0 copy-start.1
  335.8 150.9 %all-reduce.35.cloned.1.call-start = ((), (), s32[]{:S(2)}) async-start(), calls=%async_computation.9 | async-start | bytes 2228224 | tf_op jit(solution)/shard_map/psum | solution.py:9
  339.6 192.9 %all-reduce.23.cloned.1.call-start = ((), (), s32[]{:S(2)}) async-start(), calls=%async_computation.3 | async-start | bytes 262144 | tf_op jit(solution)/shard_map/psum | solution.py:9
  486.7 9.5 copy-start.4
  486.7 9.5 copy-start.13
  486.7 45.8 %copy-start.6 = (bf16[4,1,128,256]{3,2,1,0:T(8,128)(2,1)S(1)}, bf16[4,1,128,256]{3,2,1,0:T(8,128)(2,1)}, u32[]{:S(2)}) copy-start(bf16[4,1,128,256]{3,2,1,0:T(8,128)(2,1)} %param.9) | copy-start | bytes 786436
  490.6 2.0 copy-start.3
  493.5 146.5 %all-reduce.25.cloned.1.call-start = ((), (), s32[]{:S(2)}) async-start(), calls=%async_computation.4 | async-start | bytes 262144 | tf_op jit(solution)/shard_map/psum | solution.py:89
  532.5 323.0 %copy-start.5 = (bf16[4,128,128]{2,1,0:T(8,128)(2,1)S(1)}, bf16[4,128,128]{2,1,0:T(8,128)(2,1)}, u32[]{:S(2)}) copy-start(bf16[4,128,128]{2,1,0:T(8,128)(2,1)} %all-reduce.23.cloned.1.call-done) | copy-start | bytes 393220
  534.4 214.5 %all-reduce.33.cloned.1.call-start = ((), (), s32[]{:S(2)}) async-start(), calls=%async_computation.8 | async-start | bytes 2228224 | tf_op jit(solution)/shard_map/psum | solution.py:9
  535.3 318.0 %all-reduce.27.cloned.1.call-start = ((), (), s32[]{:S(2)}) async-start(), calls=%async_computation.5 | async-start | bytes 262144 | tf_op jit(solution)/shard_map/psum | solution.py:89
  751.0 206.8 %all-reduce.29.cloned.1.call-start = ((), (), s32[]{:S(2)}) async-start(), calls=%async_computation.6 | async-start | bytes 262144 | tf_op jit(solution)/shard_map/psum | solution.py:89
  855.3 206.8 %all-reduce.31.cloned.1.call-start = ((), (), s32[]{:S(2)}) async-start(), calls=%async_computation.7 | async-start | bytes 262144 | tf_op jit(solution)/shard_map/psum | solution.py:89
  855.5 104.2 %copy-start.14 = (bf16[128,256]{1,0:T(8,128)(2,1)S(1)}, bf16[128,256]{1,0:T(8,128)(2,1)}, u32[]{:S(2)}) copy-start(bf16[128,256]{1,0:T(8,128)(2,1)} %get-tuple-element.13) | copy-start | bytes 196612
  1063.1 0.7 copy-start.10
Sparse Core Ops, SparseCore 0:
  16.0 42.5 all-reduce.16
  62.7 107.9 all-reduce.38
  178.3 38.9 all-reduce.18
  221.1 107.9 all-reduce.36
  335.9 38.8 all-reduce.20
  378.8 107.9 all-reduce.34
  493.6 38.8 all-reduce.22
  536.3 103.5 all-reduce.24
  644.0 104.9 all-reduce.32
  752.6 100.6 all-reduce.26
  857.1 100.6 all-reduce.28
  961.4 100.6 all-reduce.30
where the time goes:
time: 1070 us
  waiting for transfers between devices  974 us (91%)
  matrix products  44.8 us (4%)
  between operations  29.6 us (3%)
  local copies, waits for them, and re-layouts  18 us (2%)
    psum x8, waiting for transfers between devices, spread(): return lax.psum(block, axis)  578 us
    psum x4, waiting for transfers between devices, body(): total = lax.psum(partial_sum, 'wide')  396 us
  transfers between devices with their start and end apart: 12, of which 12 were waited for; matrix products, arithmetic and copies ran while one was open for 3% of the time, Pallas kernels for 0%

commit v1 on v0

v1 whole, which is shorter than its diff:
```python
import jax
import jax.numpy as jnp
from jax import lax
from jax.experimental import pallas as pl
from jax.experimental.pallas import tpu as pltpu
from jax.sharding import PartitionSpec as P

BF = jnp.bfloat16
F32 = jnp.float32
BS = 128
NP = 4
NR = 4
NC = 32
NRHS = 256
NW = 32
PIECES = 8
CPP = NC // PIECES
SUB = 16
EXTRA = SUB + 8 + 8


def dot(a, b, ca=1, cb=0):
    return lax.dot_general(a, b, (((ca,), (cb,)), ((), ())), preferred_element_type=F32)


def ranks_of(order, w):
    rank = [sum(jnp.where(order[s] == i, s, 0) for s in range(NP)) for i in range(NP)]
    own = jnp.int32(NP)
    for i in range(NP):
        own = jnp.where(w == i, rank[i], own)
    return rank, own


def panel_kernel(order, meta, mpan, own, d1, d2, d3, got, w_ref, b_ref, y_ref,
                 lown, lpiv, zt, frhs, tpart, pan, bs, ztall):
    w, q = meta[0], meta[1]
    rank, own_rank = ranks_of(order, w)
    for d, ref in enumerate((own, d1, d2, d3)):
        pan[lax.rem(q - d + 4, 4), 0 : NR * BS] = ref[0 : NR * BS]
    for k in range(NP):
        for i in range(NP):
            for p in range(PIECES):
                pan[k, NR * BS + i * BS + p * SUB : NR * BS + i * BS + (p + 1) * SUB] = got[4 * p + i, k, 0:SUB]
    for r in range(NR):
        bs[r] = b_ref[r].astype(F32)
    for i in range(NP):
        for p in range(PIECES):
            for n in range(4):
                r0 = p * SUB + 8 * (n >> 1)
                c0 = 128 * (n & 1)
                bs[NR + i, r0 : r0 + 8, c0 : c0 + 128] = got[4 * p + i, n, SUB : SUB + 8].astype(F32)
    row_rank = [own_rank, None, None, None] + rank
    for s in range(NP):
        k = order[s]
        weight = w_ref[k]
        left = dot(pan[k], weight)
        parts = []
        for i in range(NR + NP):
            part = left[i * BS : (i + 1) * BS]
            if row_rank[i] is not None:
                part = jnp.where(row_rank[i] > s, part, 0.0)
            parts.append(part.astype(BF))
        lb = jnp.concatenate(parts, axis=0)
        lown[:, s * BS : (s + 1) * BS] = lb[: NR * BS]
        lpiv[s] = lb[NR * BS :]
        if s + 1 < NP:
            uppers = []
            for j in range(NP):
                akj = pan[j, pl.ds(pl.multiple_of(NR * BS + k * BS, BS), BS), :]
                upper = dot(weight, akj, 0, 0)
                uppers.append(jnp.where(rank[j] > s, upper, 0.0).astype(BF))
            for j in range(NP):
                prod = dot(lb, uppers[j])
                for i in range(NR + NP):
                    sl = slice(i * BS, (i + 1) * BS)
                    pan[j, sl] = (pan[j, sl].astype(F32) - mpan[i * NP + j] * prod[sl]).astype(BF)
        bk = bs[NR + k].astype(BF)
        z = dot(weight, bk, 0, 0).astype(BF)
        ztall[...] = dot(bk, weight, 0, 0).astype(BF).astype(F32)
        zt[s] = ztall[pl.ds(pl.multiple_of(w * 8, 8), 8), :]
        elim = dot(lb, z)
        for i in range(NR + NP):
            bs[i] = (bs[i] - elim[i * BS : (i + 1) * BS]).astype(BF).astype(F32)
    for r in range(NR):
        frhs[r] = bs[r].astype(BF)
    y0 = jnp.where(w < NP, jnp.zeros_like(y_ref[0]), y_ref[0])
    y = jnp.concatenate([y0] + [y_ref[r] for r in range(1, NR)], axis=0)
    tpart[...] = dot(y, lown[...], 0, 0)


def solve_kernel(order, parts, zt, lpiv, w_ref, out, xs):
    total = jnp.sum(parts[...], axis=0)
    xs[...] = jnp.zeros_like(xs)
    for s in reversed(range(NP)):
        k = order[s]
        acc = total[:, s * BS : (s + 1) * BS]
        if s + 1 < NP:
            for i in range(NP):
                acc = acc + dot(xs[i].astype(BF), lpiv[s, i * BS : (i + 1) * BS, :])
        c = (zt[s] - acc).astype(BF)
        xs[k] = dot(c, w_ref[k], 1, 1).astype(BF).astype(F32)
    x = jnp.concatenate([xs[i] for i in range(NP)], axis=1).astype(BF)
    for d in range(NW):
        out[d] = x


GC = 8


def update_kernel(order, meta, mown, mpiv, a_ref, u_ref, w_ref, lown, lpiv, out, aw, us):
    g = pl.program_id(0)
    q = meta[1]
    rank, _ = ranks_of(order, meta[0])
    qrank = jnp.int32(0)
    for i in range(NP):
        qrank = jnp.where(q == i, rank[i], qrank)
    for col in range(GC):
        for k in range(NP):
            aw[k, :, col * BS : (col + 1) * BS] = u_ref[col // CPP, k, col % CPP]
    for s in range(NP):
        k = order[s]
        upper = dot(w_ref[k], aw[k], 0, 0)
        first = jnp.where((g == 0) & (qrank <= s), 0.0, upper[:, :BS])
        ub = jnp.concatenate([first, upper[:, BS:]], axis=1).astype(BF)
        us[s * BS : (s + 1) * BS, :] = ub
        for t in range(s + 1, NP):
            k2 = order[t]
            prod = dot(lpiv[s, pl.ds(pl.multiple_of(k2 * BS, BS), BS), :], ub)
            for col in range(GC):
                sl = slice(col * BS, (col + 1) * BS)
                m = mpiv[k2 * NC + g * GC + col]
                aw[k2, :, sl] = (aw[k2, :, sl].astype(F32) - m * prod[:, sl]).astype(BF)
    rows = lax.broadcasted_iota(jnp.int32, (BS, BS), 0)
    cols = lax.broadcasted_iota(jnp.int32, (BS, BS), 1)
    perm = jnp.where((rows % GC) * SUB + rows // GC == cols, 1.0, 0.0).astype(BF)
    for r in range(NR):
        lu = dot(lown[r * BS : (r + 1) * BS, :], us[...])
        blocks = []
        for col in range(GC):
            m = mown[r * NC + g * GC + col]
            blocks.append((m * lu[:, col * BS : (col + 1) * BS]).astype(BF))
        for ag in range(BS // SUB):
            sl = slice(ag * SUB, (ag + 1) * SUB)
            stack = jnp.concatenate([b[sl] for b in blocks], axis=0)
            delta = dot(perm, stack).reshape(SUB, GC, BS)
            out[r, sl] = (a_ref[r, sl].astype(F32) - delta).astype(BF)


def vmem(n):
    return [pl.BlockSpec(memory_space=pltpu.VMEM)] * n


def smem(n):
    return [pl.BlockSpec(memory_space=pltpu.SMEM)] * n


def body(front, pivot_inverse, rhs, trail_sol, block_mask, panel_order):
    w, q = lax.axis_index("wide"), lax.axis_index("narrow")
    meta = jnp.stack([w, q]).astype(jnp.int32)
    blocks = front.reshape(NR, BS, NC, BS)
    mask = block_mask.reshape(NR, NC)
    b = rhs.reshape(NR, BS, NRHS)
    y = trail_sol.reshape(NR, BS, NRHS)

    mine = blocks[:, :, 0, :].reshape(NR * BS, BS)
    mrow = jnp.broadcast_to(jnp.pad(mask[:, :1], ((0, 4), (0, 0))).astype(BF), (8, BS))
    mine = jnp.concatenate([mine, mrow], axis=0)
    others = [lax.ppermute(mine, "narrow", [(i, (i + d) % 4) for i in range(4)]) for d in (1, 2, 3)]

    urows = blocks[0].reshape(BS, PIECES, CPP, BS).transpose(1, 2, 0, 3).reshape(PIECES, CPP * BS, BS)
    prow = blocks[0, :, 0, :].reshape(PIECES, SUB, BS)
    tiles = b[0].reshape(PIECES, 2, 8, 2, BS)
    tile = lax.dynamic_index_in_dim(tiles, q // 2, 1, keepdims=False)
    tile = lax.dynamic_index_in_dim(tile, q % 2, 2, keepdims=False)
    mline = jnp.pad(mask[0].astype(BF), (0, BS - NC))
    mline = jnp.broadcast_to(mline[None, None, :], (PIECES, 8, BS))
    groups = [[4 * p + i for p in range(PIECES)] for i in range(NP)]
    sent = jnp.concatenate([urows, prow, tile, mline], axis=1)
    got = lax.all_to_all(sent, "wide", 0, 0, axis_index_groups=groups)[0]

    ugath = lax.all_gather(got[: CPP * BS], "wide").reshape(PIECES, NP, CPP, BS, BS)

    small = jnp.broadcast_to(got[None, CPP * BS :], (NW * 4, EXTRA, BS))
    small = lax.all_to_all(small, ("wide", "narrow"), 0, 0).reshape(NW, 4, EXTRA, BS)

    mlines = small[:NP, :, SUB + 8, :NC].astype(F32)
    mpiv = lax.dynamic_index_in_dim(mlines, q, 1, keepdims=False).reshape(NP * NC)
    own_cols = jnp.stack([mine[NR * BS :, 0]] + [o[NR * BS :, 0] for o in others])[:, :NR]
    own_cols = own_cols[jnp.mod(q - jnp.arange(4), 4)]
    mpan = jnp.concatenate([own_cols.T.astype(F32), mlines[:, :, 0]], axis=0).reshape(-1)
    mown = mask.astype(F32).reshape(-1)

    lown, lpiv, zt, frhs, tpart = pl.pallas_call(
        panel_kernel,
        out_shape=(
            jax.ShapeDtypeStruct((NR * BS, NP * BS), BF),
            jax.ShapeDtypeStruct((NP, NP * BS, BS), BF),
            jax.ShapeDtypeStruct((NP, 8, BS), F32),
            jax.ShapeDtypeStruct((NR, BS, NRHS), BF),
            jax.ShapeDtypeStruct((NRHS, NP * BS), F32),
        ),
        in_specs=smem(3) + vmem(8),
        out_specs=tuple(vmem(5)),
        scratch_shapes=[
            pltpu.VMEM((NP, (NR + NP) * BS, BS), BF),
            pltpu.VMEM((NR + NP, BS, NRHS), F32),
            pltpu.VMEM((NRHS, BS), F32),
        ],
        name="panel",
    )(panel_order, meta, mpan, mine, *others, small, pivot_inverse, b, y)

    tparts = lax.all_to_all(tpart.reshape(NW, 8, NP * BS), "wide", 0, 0)
    xg = pl.pallas_call(
        solve_kernel,
        out_shape=jax.ShapeDtypeStruct((NW, 8, NP * BS), BF),
        in_specs=smem(1) + vmem(4),
        out_specs=vmem(1)[0],
        scratch_shapes=[pltpu.VMEM((NP, 8, BS), F32)],
        name="solve",
    )(panel_order, tparts, zt, lpiv, pivot_inverse)
    xall = lax.all_to_all(xg, "wide", 0, 0).reshape(NRHS, NP * BS)
    window = xall.T.reshape(NP, BS, NRHS)

    fixed2 = lambda shape: pl.BlockSpec(shape, lambda g: (0,) * len(shape))
    front_out = pl.pallas_call(
        update_kernel,
        out_shape=jax.ShapeDtypeStruct((NR, BS, NC, BS), BF),
        grid=(NC // GC,),
        in_specs=smem(4)
        + [
            pl.BlockSpec((NR, BS, GC, BS), lambda g: (0, 0, g, 0)),
            pl.BlockSpec((GC // CPP, NP, CPP, BS, BS), lambda g: (g, 0, 0, 0, 0)),
            fixed2((NP, BS, BS)),
            fixed2((NR * BS, NP * BS)),
            fixed2((NP, NP * BS, BS)),
        ],
        out_specs=pl.BlockSpec((NR, BS, GC, BS), lambda g: (0, 0, g, 0)),
        scratch_shapes=[
            pltpu.VMEM((NP, BS, GC * BS), BF),
            pltpu.VMEM((NP * BS, GC * BS), BF),
        ],
        name="update",
    )(panel_order, meta, mown, mpiv, blocks, ugath, pivot_inverse, lown, lpiv)
    return front_out.reshape(front.shape), frhs.reshape(rhs.shape), window


def solution(mesh):
    in_specs = (
        P(None, "wide", None, None, "narrow", None),
        P(),
        P(None, "wide", None, None),
        P(None, "wide", None, None),
        P(None, "wide", None, "narrow"),
        P(),
    )
    out_specs = (P(None, "wide", None, None, "narrow", None), P(None, "wide", None, None), P())
    return jax.shard_map(body, mesh=mesh, in_specs=in_specs, out_specs=out_specs, check_vma=False)
```

time: 1070 us -> 135 us (0.13)
  waiting for transfers between devices: 974 us -> 22.5 us
  matrix products: 44.8 us -> 0 us
  blocking collectives: 0 us -> 44.2 us
  Pallas kernels: 0 us -> 25.4 us
  starting transfers between devices: 0.68 us -> 16.7 us
  between operations: 29.6 us -> 14.3 us
    psum x12 -> x0, waiting for transfers between devices: 974 us -> none  [the longest x8 578 us: spread(): return lax.psum(block, axis)]
    dot_general x28 -> x0, matrix products: 44.8 us -> none  [the longest x4 18.1 us: body(): jnp.einsum('rac,cjb->rajb', left, upper, preferred_element_type=jnp.float32)]
    all_to_all x0 -> x2, blocking collectives: none -> 44.2 us  [the longest x1 24.9 us: body(): got = lax.all_to_all(sent, 'wide', 0, 0, axis_index_groups=groups)[0]]
    pallas_call x0 -> x3, Pallas kernels: none -> 25.4 us  [the longest x1 16.5 us: body(): pl.pallas_call(update_kernel, out_shape=jax.ShapeDtypeStruct((NR, BS, NC,...]
    ppermute x0 -> x3, waiting for transfers between devices: none -> 13.9 us  [body(): lax.ppermute(mine, 'narrow', [(i, (i + d) % 4) for i in range(4)])]
    unnamed x33 -> x15, local copies, waits for them, and re-layouts: 13.7 us -> 0.06 us
    all_to_all x0 -> x2, starting transfers between devices: none -> 11.7 us  [the longest x1 7.41 us: body(): lax.all_to_all(small, ('wide', 'narrow'), 0, 0).reshape(NW, 4, EXTRA, BS)]
  transfers between devices with their start and end apart: 12 -> 6, of which waited for: 12 -> 4; matrix products, arithmetic and copies ran while one was open for 3% -> 6% of each run, Pallas kernels for 0% -> 7%
where the time goes in v1:
time: 135 us; the launch traced here: 134 us
  blocking collectives  44.2 us (33%)
  Pallas kernels  25.4 us (19%)
  waiting for transfers between devices  22.5 us (17%)
  starting transfers between devices  16.7 us (12%)
  between operations  14.3 us (11%)
  local copies, waits for them, and re-layouts  10 us (7%)
    all_to_all x1, blocking collectives, body(): got = lax.all_to_all(sent, 'wide', 0, 0, axis_index_groups=groups)[0]  24.9 us
    all_to_all x1, blocking collectives, body(): tparts = lax.all_to_all(tpart.reshape(NW, 8, NP * BS), 'wide', 0, 0)  19.3 us
    pallas_call x1, Pallas kernels, body(): pl.pallas_call(update_kernel, out_shape=jax.ShapeDtypeStruct((NR, BS, NC,...  16.5 us
    ppermute x3, waiting for transfers between devices, body(): lax.ppermute(mine, 'narrow', [(i, (i + d) % 4) for i in range(4)])  13.9 us
    all_to_all x1, waiting for transfers between devices, body(): xall = lax.all_to_all(xg, 'wide', 0, 0).reshape(NRHS, NP * BS)  7.62 us
    all_to_all x1, starting transfers between devices, body(): lax.all_to_all(small, ('wide', 'narrow'), 0, 0).reshape(NW, 4, EXTRA, BS)  7.41 us
    pallas_call x1, Pallas kernels, body(): pl.pallas_call(panel_kernel, out_shape=(jax.ShapeDtypeStruct((NR * BS, NP...  5.85 us
    ppermute x3, starting transfers between devices, body(): lax.ppermute(mine, 'narrow', [(i, (i + d) % 4) for i in range(4)])  5 us
  transfers between devices with their start and end apart: 6, of which 4 were waited for; matrix products, arithmetic and copies ran while one was open for 6% of the time, Pallas kernels for 7%

profile of v1, /device:TPU:1, one launch (start us, length us, event | category | flops | bytes accessed | tf_op | source)
XLA Modules:
  0.0 134.0 jit_solution(7369938221883593691)
XLA Ops:
  7.2 0.0 copy-start.5
  7.2 0.0 all-gather.2.cloned.1.call-start
  7.3 0.0 slice-start
  7.3 1.3 slice.53
  8.6 1.0 slice.69
  9.6 0.0 copy-done.5
  9.6 0.4 copy.21
  10.1 0.0 slice-done
  10.1 0.1 pad_maximum_fusion
  10.2 24.9 %all_to_all.20 = bf16[8,544,128]{2,1,0:T(8,128)(2,1)S(1)} all-to-all(bf16[8,544,128]{2,1,0:T(8,128)(2,1)S(1)} %pad_maximum_fusion), channel_id=1, replica_groups={{0,16,32,48,64,80,96,112},{4,20,36,52,68,84,100,116},{8,24,40,56,72,88,..., dimensions={0} | all-to-all | bytes 2228224 | tf_op jit(solution)/shard_map/all_to_all | solution.py:179
  35.0 0.7 slice.73
  35.7 0.0 all-gather.2.cloned.1.call-update
  35.7 1.4 %slice.74 = bf16[4,128,1,128]{3,2,1,0:T(2,128)(2,1)S(1)} slice(bf16[4,128,32,128]{3,2,1,0:T(8,128)(2,1)} %bitcast.50), slice={[0:4], [0:128], [0:1], [0:128]} | slice | bytes 262144 | tf_op jit(solution)/shard_map/slice | solution.py:165
  37.1 0.1 pad_reduce_fusion
  37.3 1.1 broadcast_in_dim.24
  38.4 7.4 %all-to-all-start.1 = ((bf16[128,32,128]{2,1,0:T(8,128)(2,1)}), bf16[128,32,128]{2,1,0:T(8,128)(2,1)S(1)}, u32[]{:S(2)}, u32[]{:S(2)}) async-start(bf16[128,32,128]{2,1,0:T(8,128)(2,1)} %broadcast_in_dim.24), calls=%async_computation.1 | async-start | bytes 2097152 | tf_op jit(solution)/shard_map/all_to_all | solution.py:184
  45.8 0.1 pad_maximum_fusion.1.own
  45.9 0.0 copy-start.1
  46.0 1.4 %collective-permute-start = (bf16[520,128]{1,0:T(8,128)(2,1)S(1)}, bf16[520,128]{1,0:T(8,128)(2,1)S(1)}, u32[]{:S(2)}, u32[]{:S(2)}) collective-permute-start(bf16[520,128]{1,0:T(8,128)(2,1)S(1)} %pad_maximum_fusion.1.own), channel_id=1, source_target_pairs={{0,1},{1,2},{2,3},{3,0},{4,5},{5,6},{6,7},{7,4},{8,9},{9,10},{10,1... | collective-permute-start | bytes 399368 | tf_op jit(solution)/shard_map/ppermute | solution.py:168
  47.4 2.5 %collective-permute-start.1 = (bf16[520,128]{1,0:T(8,128)(2,1)S(1)}, bf16[520,128]{1,0:T(8,128)(2,1)S(1)}, u32[]{:S(2)}, u32[]{:S(2)}) collective-permute-start(bf16[520,128]{1,0:T(8,128)(2,1)S(1)} %pad_maximum_fusion.1.own), channel_id=1, source_target_pairs={{0,2},{1,3},{2,0},{3,1},{4,6},{5,7},{6,4},{7,5},{8,10},{9,11},{10,... | collective-permute-start | bytes 399368 | tf_op jit(solution)/shard_map/ppermute | solution.py:168
  49.8 1.1 collective-permute-start.2
  51.0 0.6 pad_add_fusion.meta
  51.6 8.6 %collective-permute-done.d1 = bf16[520,128]{1,0:T(8,128)(2,1)S(1)} collective-permute-done((bf16[520,128]{1,0:T(8,128)(2,1)S(1)}, bf16[520,128]{1,0:T(8,128)(2,1)S(1)}, u32[]{:S(2)}, u32[]{:S(2)}) %collective-permute-start) | collective-permute-done | bytes 133152 | tf_op jit(solution)/shard_map/ppermute | solution.py:168
  60.1 0.1 slice_reduce_fusion.2
  60.3 5.4 %collective-permute-done.1.d2 = bf16[520,128]{1,0:T(8,128)(2,1)S(1)} collective-permute-done((bf16[520,128]{1,0:T(8,128)(2,1)S(1)}, bf16[520,128]{1,0:T(8,128)(2,1)S(1)}, u32[]{:S(2)}, u32[]{:S(2)}) %collective-permute-start.1) | collective-permute-done | bytes 133152 | tf_op jit(solution)/shard_map/ppermute | solution.py:168
  65.6 0.1 slice_reduce_fusion.1
  65.7 0.0 collective-permute-done.2.d3
  65.8 0.1 slice_reduce_fusion
  65.9 0.6 gather_fusion
  66.5 1.0 all-to-all-done.1
  67.4 0.1 copy.28
  67.5 0.1 pad_maximum_fusion.2
  67.6 0.1 copy.24
  67.7 0.7 reshape.127.mpan
  68.4 0.0 copy-done.1
  68.4 0.0 copy-done.2
  68.4 0.0 copy-done.3
  68.4 0.0 copy-done.4
  68.4 0.0 copy-done
  68.4 5.8 %panel.1 = (bf16[512,512]{1,0:T(8,128)(2,1)}, bf16[4,512,128]{2,1,0:T(8,128)(2,1)}, f32[4,8,128]{2,1,0:T(8,128)}, bf16[4,128,256]{2,1,0:T(8,128)(2,1)}, f32[256,512]{1,0:T(8,128)}) custom-call(s32[4]{0:T(128)} %order.5, s32[2]{0:T(128)} %pad_add_fusion.meta, f32[32]{0:T(128)} %reshape.127.mpan, bf16[520,128]{1,0:T(8,128)(2,1)} %copy-done.1, ...), custom_call_target="tpu_custom_call" | custom-call | tf_op jit(solution)/shard_map/panel/pallas_call | solution.py:193
  74.3 19.3 %all_to_all.21.parts = f32[32,8,512]{2,1,0:T(8,128)} all-to-all(f32[32,8,512]{2,1,0:T(8,128)} %bitcast.60), channel_id=1, replica_groups=mesh['wide'=32,'narrow'=4] {'wide'}, dimensions={0} | all-to-all | bytes 1048576 | tf_op jit(solution)/shard_map/all_to_all | solution.py:212
  93.6 3.0 %solve.1 = bf16[32,8,512]{2,1,0:T(8,128)(2,1)} custom-call(s32[4]{0:T(128)} %order.5, f32[32,8,512]{2,1,0:T(8,128)} %all_to_all.21.parts, f32[4,8,128]{2,1,0:T(8,128)} %get-tuple-element.12.zt, bf16[4,512,128]{2,1,0:T(8,128)(2,1)} %get-tuple-element.9.lpiv, bf16[4,128,128]{2,1,0:T(8,128)(2,1)} %w_ref.5), custom_call_target="tpu_custom_call" | custom-call | tf_op jit(solution)/shard_map/solve/pallas_call | solution.py:213
  96.6 4.3 %all-to-all-start.3 = ((bf16[32,8,512]{2,1,0:T(8,128)(2,1)}), bf16[32,8,512]{2,1,0:T(8,128)(2,1)S(1)}, u32[]{:S(2)}, u32[]{:S(2)}) async-start(bf16[32,8,512]{2,1,0:T(8,128)(2,1)} %solve.1), calls=%async_computation.3 | async-start | bytes 524288 | tf_op jit(solution)/shard_map/all_to_all | solution.py:221
  100.9 0.6 convert_element_type.27.mown
  101.5 0.7 reshape.124.mpiv
  102.2 7.6 %all-to-all-done.3 = bf16[32,8,512]{2,1,0:T(8,128)(2,1)S(1)} async-done(((bf16[32,8,512]{2,1,0:T(8,128)(2,1)}), bf16[32,8,512]{2,1,0:T(8,128)(2,1)S(1)}, u32[]{:S(2)}, u32[]{:S(2)}) %all-to-all-start.3) | async-done | bytes 262176 | tf_op jit(solution)/shard_map/all_to_all | solution.py:221
  109.8 0.8 copy.25
  110.6 16.5 %update.1 = bf16[4,128,32,128]{3,2,1,0:T(8,128)(2,1)} custom-call(s32[4]{0:T(128)} %order.5, s32[2]{0:T(128)} %pad_add_fusion.meta, f32[128]{0:T(128)} %convert_element_type.27.mown, f32[128]{0:T(128)} %reshape.124.mpiv, bf16[4,128,32,128]{3,2,1,0:T(8,128)(2,1)} %bitcast.51, bf16[8,4,4,128,128]{4,3,2,1,0:T(8,128)(2,1)} %bitcast.54, ...), custom_call_target="tpu_custom_call" | custom-call | tf_op jit(solution)/shard_map/update/pallas_call | solution.py:225
  (22 shorter events, 0.2 us)
Async XLA Ops:
  7.2 2.4 %copy-start.5 = (s32[4,1,32,1]{2,3,1,0:T(1,128)S(1)}, s32[4,1,32,1]{2,3,1,0:T(1,128)}, u32[]{:S(2)}) copy-start(s32[4,1,32,1]{2,3,1,0:T(1,128)} %param.10) | copy-start | bytes 1540
  7.2 103.5 %all-gather.2.cloned.1.call-start = ((), (), s32[]{:S(2)}) async-start(), calls=%async_computation.4 | async-start | bytes 4325376 | tf_op jit(solution)/shard_map/all_gather | solution.py:181
  7.3 2.8 %slice-start = ((bf16[4,1,128,256]{3,2,1,0:T(8,128)(2,1)}), bf16[1,1,128,256]{3,2,1,0:T(8,128)(2,1)S(1)}, s32[]{:S(2)}) async-start(bf16[4,1,128,256]{3,2,1,0:T(8,128)(2,1)} %param.8), calls=%async_computation.5 | async-start | bytes 131072 | tf_op jit(solution)/shard_map/slice | solution.py:172
  38.4 29.0 %all-to-all-start.1 = ((bf16[128,32,128]{2,1,0:T(8,128)(2,1)}), bf16[128,32,128]{2,1,0:T(8,128)(2,1)S(1)}, u32[]{:S(2)}, u32[]{:S(2)}) async-start(bf16[128,32,128]{2,1,0:T(8,128)(2,1)} %broadcast_in_dim.24), calls=%async_computation.1 | async-start | bytes 2097152 | tf_op jit(solution)/shard_map/all_to_all | solution.py:184
  45.9 22.5 %copy-start.1 = (bf16[520,128]{1,0:T(8,128)(2,1)}, bf16[520,128]{1,0:T(8,128)(2,1)S(1)}, u32[]{:S(2)}) copy-start(bf16[520,128]{1,0:T(8,128)(2,1)S(1)} %pad_maximum_fusion.1.own) | copy-start | bytes 399364
  46.0 14.2 %collective-permute-start = (bf16[520,128]{1,0:T(8,128)(2,1)S(1)}, bf16[520,128]{1,0:T(8,128)(2,1)S(1)}, u32[]{:S(2)}, u32[]{:S(2)}) collective-permute-start(bf16[520,128]{1,0:T(8,128)(2,1)S(1)} %pad_maximum_fusion.1.own), channel_id=1, source_target_pairs={{0,1},{1,2},{2,3},{3,0},{4,5},{5,6},{6,7},{7,4},{8,9},{9,10},{10,1... | collective-permute-start | bytes 399368 | tf_op jit(solution)/shard_map/ppermute | solution.py:168
  47.4 18.2 %collective-permute-start.1 = (bf16[520,128]{1,0:T(8,128)(2,1)S(1)}, bf16[520,128]{1,0:T(8,128)(2,1)S(1)}, u32[]{:S(2)}, u32[]{:S(2)}) collective-permute-start(bf16[520,128]{1,0:T(8,128)(2,1)S(1)} %pad_maximum_fusion.1.own), channel_id=1, source_target_pairs={{0,2},{1,3},{2,0},{3,1},{4,6},{5,7},{6,4},{7,5},{8,10},{9,11},{10,... | collective-permute-start | bytes 399368 | tf_op jit(solution)/shard_map/ppermute | solution.py:168
  49.8 15.9 %collective-permute-start.2 = (bf16[520,128]{1,0:T(8,128)(2,1)S(1)}, bf16[520,128]{1,0:T(8,128)(2,1)S(1)}, u32[]{:S(2)}, u32[]{:S(2)}) collective-permute-start(bf16[520,128]{1,0:T(8,128)(2,1)S(1)} %pad_maximum_fusion.1.own), channel_id=1, source_target_pairs={{0,3},{1,0},{2,1},{3,2},{4,7},{5,4},{6,5},{7,6},{8,11},{9,8},{10,9... | collective-permute-start | bytes 399368 | tf_op jit(solution)/shard_map/ppermute | solution.py:168
  60.1 8.3 %copy-start.2 = (bf16[520,128]{1,0:T(8,128)(2,1)}, bf16[520,128]{1,0:T(8,128)(2,1)S(1)}, u32[]{:S(2)}) copy-start(bf16[520,128]{1,0:T(8,128)(2,1)S(1)} %collective-permute-done.d1) | copy-start | bytes 399364
  65.6 2.8 %copy-start.3 = (bf16[520,128]{1,0:T(8,128)(2,1)}, bf16[520,128]{1,0:T(8,128)(2,1)S(1)}, u32[]{:S(2)}) copy-start(bf16[520,128]{1,0:T(8,128)(2,1)S(1)} %collective-permute-done.1.d2) | copy-start | bytes 399364
  65.7 2.7 %copy-start.4 = (bf16[520,128]{1,0:T(8,128)(2,1)}, bf16[520,128]{1,0:T(8,128)(2,1)S(1)}, u32[]{:S(2)}) copy-start(bf16[520,128]{1,0:T(8,128)(2,1)S(1)} %collective-permute-done.2.d3) | copy-start | bytes 399364
  67.4 1.0 copy-start
  96.6 13.2 %all-to-all-start.3 = ((bf16[32,8,512]{2,1,0:T(8,128)(2,1)}), bf16[32,8,512]{2,1,0:T(8,128)(2,1)S(1)}, u32[]{:S(2)}, u32[]{:S(2)}) async-start(bf16[32,8,512]{2,1,0:T(8,128)(2,1)} %solve.1), calls=%async_computation.3 | async-start | bytes 524288 | tf_op jit(solution)/shard_map/all_to_all | solution.py:221
Sparse Core Ops, SparseCore 0:
  35.9 55.8 all-gather.1

commit v2 on v1

--- a/solution.py
+++ b/solution.py
@@ -19,6 +19,11 @@
 EXTRA = SUB + 8 + 8
 
 
+def holder(p, i):
+    z = i >> 1 if p % 2 == 0 else 3 - (i >> 1)
+    return (p >> 1) * 8 + z * 2 + (i & 1)
+
+
 def dot(a, b, ca=1, cb=0):
     return lax.dot_general(a, b, (((ca,), (cb,)), ((), ())), preferred_element_type=F32)
 
@@ -32,7 +37,7 @@
 
 
 def panel_kernel(order, meta, mpan, own, d1, d2, d3, got, w_ref, b_ref, y_ref,
-                 lown, lpiv, zt, frhs, tpart, pan, bs, ztall):
+                 lown, lpiv, zt, frhs, tpart, delta, pan, bs, ztall):
     w, q = meta[0], meta[1]
     rank, own_rank = ranks_of(order, w)
     for d, ref in enumerate((own, d1, d2, d3)):
@@ -40,7 +45,7 @@
     for k in range(NP):
         for i in range(NP):
             for p in range(PIECES):
-                pan[k, NR * BS + i * BS + p * SUB : NR * BS + i * BS + (p + 1) * SUB] = got[4 * p + i, k, 0:SUB]
+                pan[k, NR * BS + i * BS + p * SUB : NR * BS + i * BS + (p + 1) * SUB] = got[holder(p, i), k, 0:SUB]
     for r in range(NR):
         bs[r] = b_ref[r].astype(F32)
     for i in range(NP):
@@ -48,7 +53,7 @@
             for n in range(4):
                 r0 = p * SUB + 8 * (n >> 1)
                 c0 = 128 * (n & 1)
-                bs[NR + i, r0 : r0 + 8, c0 : c0 + 128] = got[4 * p + i, n, SUB : SUB + 8].astype(F32)
+                bs[NR + i, r0 : r0 + 8, c0 : c0 + 128] = got[holder(p, i), n, SUB : SUB + 8].astype(F32)
     row_rank = [own_rank, None, None, None] + rank
     for s in range(NP):
         k = order[s]
@@ -83,6 +88,7 @@
             bs[i] = (bs[i] - elim[i * BS : (i + 1) * BS]).astype(BF).astype(F32)
     for r in range(NR):
         frhs[r] = bs[r].astype(BF)
+    delta[...] = (own[0 : NR * BS].astype(F32) - pan[q, 0 : NR * BS].astype(F32)).astype(BF)
     y0 = jnp.where(w < NP, jnp.zeros_like(y_ref[0]), y_ref[0])
     y = jnp.concatenate([y0] + [y_ref[r] for r in range(1, NR)], axis=0)
     tpart[...] = dot(y, lown[...], 0, 0)
@@ -104,46 +110,64 @@
         out[d] = x
 
 
+def combine_kernel(order, lown, lpiv, w_ref, h):
+    def low(t, s):
+        return lpiv[s, pl.ds(pl.multiple_of(order[t] * BS, BS), BS), :]
+
+    def right(coeff, s):
+        return dot(coeff.astype(BF), w_ref[order[s]], 1, 1).astype(BF)
+
+    base = [lown[:, s * BS : (s + 1) * BS].astype(F32) for s in range(NP)]
+    r3 = right(base[3], 3)
+    r3_low = [dot(r3, low(3, s)) for s in range(3)]
+    for m3 in range(2):
+        c3 = [base[s] - r3_low[s] if m3 else base[s] for s in range(3)]
+        r2 = right(c3[2], 2)
+        r2_low = [dot(r2, low(2, s)) for s in range(2)]
+        for m2 in range(2):
+            c2 = [c3[s] - r2_low[s] if m2 else c3[s] for s in range(2)]
+            r1 = right(c2[1], 1)
+            r1_low = dot(r1, low(1, 0))
+            for m1 in range(2):
+                r0 = right(c2[0] - r1_low if m1 else c2[0], 0)
+                pat = m1 + 2 * m2 + 4 * m3
+                for s, block in enumerate((r0, r1, r2, r3)):
+                    h[pat, :, s * BS : (s + 1) * BS] = block
+
+
 GC = 8
 
 
-def update_kernel(order, meta, mown, mpiv, a_ref, u_ref, w_ref, lown, lpiv, out, aw, us):
+def update_kernel(order, meta, mown, mpiv, a_ref, near, far, h, delta, out, rows_of):
     g = pl.program_id(0)
-    q = meta[1]
-    rank, _ = ranks_of(order, meta[0])
-    qrank = jnp.int32(0)
-    for i in range(NP):
-        qrank = jnp.where(q == i, rank[i], qrank)
-    for col in range(GC):
-        for k in range(NP):
-            aw[k, :, col * BS : (col + 1) * BS] = u_ref[col // CPP, k, col % CPP]
-    for s in range(NP):
-        k = order[s]
-        upper = dot(w_ref[k], aw[k], 0, 0)
-        first = jnp.where((g == 0) & (qrank <= s), 0.0, upper[:, :BS])
-        ub = jnp.concatenate([first, upper[:, BS:]], axis=1).astype(BF)
-        us[s * BS : (s + 1) * BS, :] = ub
-        for t in range(s + 1, NP):
-            k2 = order[t]
-            prod = dot(lpiv[s, pl.ds(pl.multiple_of(k2 * BS, BS), BS), :], ub)
-            for col in range(GC):
-                sl = slice(col * BS, (col + 1) * BS)
-                m = mpiv[k2 * NC + g * GC + col]
-                aw[k2, :, sl] = (aw[k2, :, sl].astype(F32) - m * prod[:, sl]).astype(BF)
+    core = meta[0] & 1
+    for zg in range(2):
+        for fz in range(2):
+            z = zg if fz == 0 else 3 - zg
+            for cc in range(CPP):
+                rows_of[2 * zg + core, fz * CPP + cc] = near[0, z, cc]
+                rows_of[2 * zg + 1 - core, fz * CPP + cc] = far[0, z, cc]
     rows = lax.broadcasted_iota(jnp.int32, (BS, BS), 0)
     cols = lax.broadcasted_iota(jnp.int32, (BS, BS), 1)
     perm = jnp.where((rows % GC) * SUB + rows // GC == cols, 1.0, 0.0).astype(BF)
+    cols_out = []
+    for col in range(GC):
+        c = g * GC + col
+        pat = mpiv[order[1] * NC + c] + 2 * mpiv[order[2] * NC + c] + 4 * mpiv[order[3] * NC + c]
+        raw = jnp.concatenate([rows_of[order[s], col] for s in range(NP)], axis=0)
+        lu = dot(h[pat], raw)
+        parts = []
+        for r in range(NR):
+            parts.append(jnp.where(mown[r * NC + c] != 0, lu[r * BS : (r + 1) * BS], 0.0).astype(BF))
+        if col == 0:
+            parts = [jnp.where(g == 0, delta[r * BS : (r + 1) * BS], parts[r]) for r in range(NR)]
+        cols_out.append(parts)
     for r in range(NR):
-        lu = dot(lown[r * BS : (r + 1) * BS, :], us[...])
-        blocks = []
-        for col in range(GC):
-            m = mown[r * NC + g * GC + col]
-            blocks.append((m * lu[:, col * BS : (col + 1) * BS]).astype(BF))
         for ag in range(BS // SUB):
             sl = slice(ag * SUB, (ag + 1) * SUB)
-            stack = jnp.concatenate([b[sl] for b in blocks], axis=0)
-            delta = dot(perm, stack).reshape(SUB, GC, BS)
-            out[r, sl] = (a_ref[r, sl].astype(F32) - delta).astype(BF)
+            stack = jnp.concatenate([cols_out[col][r][sl] for col in range(GC)], axis=0)
+            change = dot(perm, stack).reshape(SUB, GC, BS)
+            out[r, sl] = (a_ref[r, sl].astype(F32) - change).astype(BF)
 
 
 def vmem(n):
@@ -174,23 +198,27 @@
     tile = lax.dynamic_index_in_dim(tile, q % 2, 2, keepdims=False)
     mline = jnp.pad(mask[0].astype(BF), (0, BS - NC))
     mline = jnp.broadcast_to(mline[None, None, :], (PIECES, 8, BS))
-    groups = [[4 * p + i for p in range(PIECES)] for i in range(NP)]
+    groups = [[holder(p, i) for p in range(PIECES)] for i in range(NP)]
     sent = jnp.concatenate([urows, prow, tile, mline], axis=1)
     got = lax.all_to_all(sent, "wide", 0, 0, axis_index_groups=groups)[0]
 
-    ugath = lax.all_gather(got[: CPP * BS], "wide").reshape(PIECES, NP, CPP, BS, BS)
+    same_core = [[v for v in range(NW) if v % 2 == c] for c in range(2)]
+    copies = jnp.broadcast_to(got[None, : CPP * BS], (NW // 2, CPP * BS, BS))
+    near = lax.all_to_all(copies, "wide", 0, 0, axis_index_groups=same_core)
+    near = near.reshape(4, 4, CPP, BS, BS)
+    far = lax.ppermute(near, "wide", [(v, v ^ 1) for v in range(NW)])
 
     small = jnp.broadcast_to(got[None, CPP * BS :], (NW * 4, EXTRA, BS))
     small = lax.all_to_all(small, ("wide", "narrow"), 0, 0).reshape(NW, 4, EXTRA, BS)
 
-    mlines = small[:NP, :, SUB + 8, :NC].astype(F32)
-    mpiv = lax.dynamic_index_in_dim(mlines, q, 1, keepdims=False).reshape(NP * NC)
+    mlines = small[:NP, :, SUB + 8, :NC]
+    mpiv = lax.dynamic_index_in_dim(mlines, q, 1, keepdims=False).reshape(NP * NC).astype(jnp.int32)
     own_cols = jnp.stack([mine[NR * BS :, 0]] + [o[NR * BS :, 0] for o in others])[:, :NR]
     own_cols = own_cols[jnp.mod(q - jnp.arange(4), 4)]
-    mpan = jnp.concatenate([own_cols.T.astype(F32), mlines[:, :, 0]], axis=0).reshape(-1)
-    mown = mask.astype(F32).reshape(-1)
-
-    lown, lpiv, zt, frhs, tpart = pl.pallas_call(
+    mpan = jnp.concatenate([own_cols.T.astype(F32), mlines[:, :, 0].astype(F32)], axis=0).reshape(-1)
+    mown = mask.reshape(-1)
+
+    lown, lpiv, zt, frhs, tpart, delta = pl.pallas_call(
         panel_kernel,
         out_shape=(
             jax.ShapeDtypeStruct((NR * BS, NP * BS), BF),
@@ -198,9 +226,10 @@
             jax.ShapeDtypeStruct((NP, 8, BS), F32),
             jax.ShapeDtypeStruct((NR, BS, NRHS), BF),
             jax.ShapeDtypeStruct((NRHS, NP * BS), F32),
+            jax.ShapeDtypeStruct((NR * BS, BS), BF),
         ),
         in_specs=smem(3) + vmem(8),
-        out_specs=tuple(vmem(5)),
+        out_specs=tuple(vmem(6)),
         scratch_shapes=[
             pltpu.VMEM((NP, (NR + NP) * BS, BS), BF),
             pltpu.VMEM((NR + NP, BS, NRHS), F32),
@@ -221,6 +250,14 @@
     xall = lax.all_to_all(xg, "wide", 0, 0).reshape(NRHS, NP * BS)
     window = xall.T.reshape(NP, BS, NRHS)
 
+    h = pl.pallas_call(
+        combine_kernel,
+        out_shape=jax.ShapeDtypeStruct((8, NR * BS, NP * BS), BF),
+        in_specs=smem(1) + vmem(3),
+        out_specs=vmem(1)[0],
+        name="combine",
+    )(panel_order, lown, lpiv, pivot_inverse)
+
     fixed2 = lambda shape: pl.BlockSpec(shape, lambda g: (0,) * len(shape))
     front_out = pl.pallas_call(
         update_kernel,
@@ -229,18 +266,15 @@
         in_specs=smem(4)
         + [
             pl.BlockSpec((NR, BS, GC, BS), lambda g: (0, 0, g, 0)),
-            pl.BlockSpec((GC // CPP, NP, CPP, BS, BS), lambda g: (g, 0, 0, 0, 0)),
-            fixed2((NP, BS, BS)),
-            fixed2((NR * BS, NP * BS)),
-            fixed2((NP, NP * BS, BS)),
+            pl.BlockSpec((1, 4, CPP, BS, BS), lambda g: (g, 0, 0, 0, 0)),
+            pl.BlockSpec((1, 4, CPP, BS, BS), lambda g: (g, 0, 0, 0, 0)),
+            fixed2((8, NR * BS, NP * BS)),
+            fixed2((NR * BS, BS)),
         ],
         out_specs=pl.BlockSpec((NR, BS, GC, BS), lambda g: (0, 0, g, 0)),
-        scratch_shapes=[
-            pltpu.VMEM((NP, BS, GC * BS), BF),
-            pltpu.VMEM((NP * BS, GC * BS), BF),
-        ],
+        scratch_shapes=[pltpu.VMEM((NP, GC, BS, BS), BF)],
         name="update",
-    )(panel_order, meta, mown, mpiv, blocks, ugath, pivot_inverse, lown, lpiv)
+    )(panel_order, meta, mown, mpiv, blocks, near, far, h, delta)
     return front_out.reshape(front.shape), frhs.reshape(rhs.shape), window
 
 

time: 135 us -> 151 us (1.12)
  blocking collectives: 44.2 us -> 73 us
  between operations: 14.3 us -> 0.86 us
  waiting for transfers between devices: 22.5 us -> 15.4 us
  other arithmetic: 0.96 us -> 6.05 us
  local copies, waits for them, and re-layouts: 10 us -> 13.4 us
    all_to_all x0 -> x1, blocking collectives: none -> 28.9 us  [body(): near = lax.all_to_all(copies, 'wide', 0, 0, axis_index_groups=same_core)]
    all_to_all x1, waiting for transfers between devices: 7.62 us -> 1.95 us  [body(): xall = lax.all_to_all(xg, 'wide', 0, 0).reshape(NRHS, NP * BS)]
    pallas_call x1, Pallas kernels: 16.5 us -> 10.9 us  [body(): pl.pallas_call(update_kernel, out_shape=jax.ShapeDtypeStruct((NR, BS, NC,...]
    pallas_call x0 -> x1, Pallas kernels: none -> 4.99 us  [body(): pl.pallas_call(combine_kernel, out_shape=jax.ShapeDtypeStruct((8, NR * BS...]
    ppermute x0 -> x1, starting transfers between devices: none -> 3.04 us  [body(): far = lax.ppermute(near, 'wide', [(v, v ^ 1) for v in range(NW)])]
    another operation x1, other arithmetic: 0.01 us -> 2.01 us
    all_to_all x1, starting transfers between devices: 7.41 us -> 5.69 us  [body(): lax.all_to_all(small, ('wide', 'narrow'), 0, 0).reshape(NW, 4, EXTRA, BS)]
  transfers between devices with their start and end apart: 6 -> 6, of which waited for: 4 -> 4; matrix products, arithmetic and copies ran while one was open for 6% -> 9% of each run, Pallas kernels for 7% -> 9%
where the time goes in v2:
time: 151 us; the launch traced here: 150 us
  blocking collectives  73 us (48%)
  Pallas kernels  24.8 us (16%)
  starting transfers between devices  16.2 us (11%)
  waiting for transfers between devices  15.4 us (10%)
  local copies, waits for them, and re-layouts  13.4 us (9%)
  other arithmetic  6.05 us (4%)
    all_to_all x1, blocking collectives, body(): near = lax.all_to_all(copies, 'wide', 0, 0, axis_index_groups=same_core)  28.9 us
    all_to_all x1, blocking collectives, body(): got = lax.all_to_all(sent, 'wide', 0, 0, axis_index_groups=groups)[0]  24.7 us
    all_to_all x1, blocking collectives, body(): tparts = lax.all_to_all(tpart.reshape(NW, 8, NP * BS), 'wide', 0, 0)  19.4 us
    ppermute x3, waiting for transfers between devices, body(): lax.ppermute(mine, 'narrow', [(i, (i + d) % 4) for i in range(4)])  13.4 us
    pallas_call x1, Pallas kernels, body(): pl.pallas_call(update_kernel, out_shape=jax.ShapeDtypeStruct((NR, BS, NC,...  10.9 us
    pallas_call x1, Pallas kernels, body(): pl.pallas_call(panel_kernel, out_shape=(jax.ShapeDtypeStruct((NR * BS, NP...  5.9 us
    all_to_all x1, starting transfers between devices, body(): lax.all_to_all(small, ('wide', 'narrow'), 0, 0).reshape(NW, 4, EXTRA, BS)  5.69 us
    pallas_call x1, Pallas kernels, body(): pl.pallas_call(combine_kernel, out_shape=jax.ShapeDtypeStruct((8, NR * BS...  4.99 us
  transfers between devices with their start and end apart: 6, of which 4 were waited for; matrix products, arithmetic and copies ran while one was open for 9% of the time, Pallas kernels for 9%

profile of v2, /device:TPU:1, one launch (start us, length us, event | category | flops | bytes accessed | tf_op | source)
XLA Modules:
  0.0 149.7 jit_solution(13037408940169282094)
XLA Ops:
  0.7 0.5 broadcast.91
  1.2 2.0 %fusion.2 = (bf16[4,1,32,1]{2,3,1,0:T(2,128)(2,1)S(1)}, s32[4,32]{1,0:T(4,128)}) fusion(s32[4,1,32,1]{2,3,1,0:T(1,128)} %param.10, s32[]{:T(128)} %broadcast.91), kind=kLoop, calls=%fused_computation.24 | loop fusion | flops 128 | bytes 1284 | tf_op jit(solution)/shard_map/convert.9
  3.2 1.3 slice.53
  4.5 1.0 slice.69
  5.5 0.4 copy.14
  6.0 0.0 slice-done
  6.0 0.1 pad_maximum_fusion
  6.1 24.7 %all_to_all.25 = bf16[8,544,128]{2,1,0:T(8,128)(2,1)S(1)} all-to-all(bf16[8,544,128]{2,1,0:T(8,128)(2,1)S(1)} %pad_maximum_fusion), channel_id=1, replica_groups={{0,24,32,56,64,88,96,120},{4,28,36,60,68,92,100,124},{8,16,40,48,72,80,..., dimensions={0} | all-to-all | bytes 2228224 | tf_op jit(solution)/shard_map/all_to_all | solution.py:203
  30.8 0.4 broadcast_in_dim.34
  31.2 28.9 %all_to_all.26 = bf16[16,512,128]{2,1,0:T(8,128)(2,1)S(1)} all-to-all(bf16[16,512,128]{2,1,0:T(8,128)(2,1)S(1)} %broadcast_in_dim.34), channel_id=1, replica_groups={{0,8,16,24,32,40,48,56,64,72,80,88,96,104,112,120},{4,12,20,28,36,44,52..., dimensions={0} | all-to-all | bytes 4194304 | tf_op jit(solution)/shard_map/all_to_all | solution.py:207
  60.1 3.0 %collective-permute-start = (bf16[4,4,4,128,128]{4,3,2,1,0:T(8,128)(2,1)S(1)}, bf16[4,4,4,128,128]{4,3,2,1,0:T(8,128)(2,1)}, u32[]{:S(2)}, u32[]{:S(2)}) collective-permute-start(bf16[4,4,4,128,128]{4,3,2,1,0:T(8,128)(2,1)S(1)} %bitcast.54), channel_id=1, source_target_pairs={{0,4},{4,0},{8,12},{12,8},{16,20},{20,16},{24,28},{28,24},{32,36},... | collective-permute-start | bytes 6291464 | tf_op jit(solution)/shard_map/ppermute | solution.py:209
  63.2 1.1 broadcast_in_dim.32
  64.3 5.7 %all-to-all-start.1 = ((bf16[128,32,128]{2,1,0:T(8,128)(2,1)}), bf16[128,32,128]{2,1,0:T(8,128)(2,1)S(1)}, u32[]{:S(2)}, u32[]{:S(2)}) async-start(bf16[128,32,128]{2,1,0:T(8,128)(2,1)} %broadcast_in_dim.32), calls=%async_computation.1 | async-start | bytes 2097152 | tf_op jit(solution)/shard_map/all_to_all | solution.py:212
  70.0 1.4 slice.74
  71.3 0.1 pad_reduce_fusion
  71.5 0.1 pad_maximum_fusion.1.own
  71.7 0.0 copy-start.2
  71.7 2.7 %collective-permute-start.3 = (bf16[520,128]{1,0:T(8,128)(2,1)S(1)}, bf16[520,128]{1,0:T(8,128)(2,1)S(1)}, u32[]{:S(2)}, u32[]{:S(2)}) collective-permute-start(bf16[520,128]{1,0:T(8,128)(2,1)S(1)} %pad_maximum_fusion.1.own), channel_id=1, source_target_pairs={{0,3},{1,0},{2,1},{3,2},{4,7},{5,4},{6,5},{7,6},{8,11},{9,8},{10,9... | collective-permute-start | bytes 399368 | tf_op jit(solution)/shard_map/ppermute | solution.py:192
  74.4 0.5 collective-permute-start.2
  74.9 0.6 collective-permute-start.1
  75.5 0.6 pad_clamp_fusion
  76.1 0.6 pad_add_fusion.meta
  76.7 8.9 %collective-permute-done.3.d3 = bf16[520,128]{1,0:T(8,128)(2,1)S(1)} collective-permute-done((bf16[520,128]{1,0:T(8,128)(2,1)S(1)}, bf16[520,128]{1,0:T(8,128)(2,1)S(1)}, u32[]{:S(2)}, u32[]{:S(2)}) %collective-permute-start.3) | collective-permute-done | bytes 133152 | tf_op jit(solution)/shard_map/ppermute | solution.py:192
  85.5 0.1 slice_reduce_fusion
  85.7 1.5 collective-permute-done.2.d2
  87.1 0.1 slice_reduce_fusion.1
  87.3 3.1 %collective-permute-done.1.d1 = bf16[520,128]{1,0:T(8,128)(2,1)} collective-permute-done((bf16[520,128]{1,0:T(8,128)(2,1)S(1)}, bf16[520,128]{1,0:T(8,128)(2,1)}, u32[]{:S(2)}, u32[]{:S(2)}) %collective-permute-start.1) | collective-permute-done | bytes 133152 | tf_op jit(solution)/shard_map/ppermute | solution.py:192
  90.3 0.8 slice_reduce_fusion.2
  91.1 0.6 pad_maximum_fusion.2
  91.7 1.3 gather_fusion
  93.0 0.0 all-to-all-done.1
  93.0 0.6 copy-done.5
  93.6 0.7 copy.21
  94.3 1.3 maximum_convert_fusion
  95.7 0.8 copy.17
  96.4 0.6 reshape.137.mpan
  97.0 5.9 %panel.1 = (bf16[512,512]{1,0:T(8,128)(2,1)}, bf16[4,512,128]{2,1,0:T(8,128)(2,1)}, f32[4,8,128]{2,1,0:T(8,128)}, bf16[4,128,256]{2,1,0:T(8,128)(2,1)}, f32[256,512]{1,0:T(8,128)}, /*index=5*/bf16[512,128]{1,0:T(8,128)(2,1)}) custom-call(s32[4]{0:T(128)} %order.7, s32[2]{0:T(128)} %pad_add_fusion.meta, f32[32]{0:T(128)} %reshape.137.mpan, ...), custom_call_target="tpu_custom_call" | custom-call | tf_op jit(solution)/shard_map/panel/pallas_call | solution.py:221
  102.9 19.4 %all_to_all.27.parts = f32[32,8,512]{2,1,0:T(8,128)} all-to-all(f32[32,8,512]{2,1,0:T(8,128)} %bitcast.65), channel_id=1, replica_groups=mesh['wide'=32,'narrow'=4] {'wide'}, dimensions={0} | all-to-all | bytes 1048576 | tf_op jit(solution)/shard_map/all_to_all | solution.py:241
  122.3 3.0 %solve.1 = bf16[32,8,512]{2,1,0:T(8,128)(2,1)} custom-call(s32[4]{0:T(128)} %order.7, f32[32,8,512]{2,1,0:T(8,128)} %all_to_all.27.parts, f32[4,8,128]{2,1,0:T(8,128)} %get-tuple-element.14.zt, bf16[4,512,128]{2,1,0:T(8,128)(2,1)} %get-tuple-element.10.lpiv, bf16[4,128,128]{2,1,0:T(8,128)(2,1)} %w_ref.5), custom_call_target="tpu_custom_call" | custom-call | tf_op jit(solution)/shard_map/solve/pallas_call | solution.py:242
  125.3 3.7 %all-to-all-start.4 = ((bf16[32,8,512]{2,1,0:T(8,128)(2,1)}), bf16[32,8,512]{2,1,0:T(8,128)(2,1)S(1)}, u32[]{:S(2)}, u32[]{:S(2)}) async-start(bf16[32,8,512]{2,1,0:T(8,128)(2,1)} %solve.1), calls=%async_computation.4 | async-start | bytes 524288 | tf_op jit(solution)/shard_map/all_to_all | solution.py:250
  129.0 0.7 reshape_reshape.3.mown
  129.7 0.7 convert_reduce_fusion
  130.4 0.6 reshape.135.mpiv
  131.0 5.0 %combine.1.h = bf16[8,512,512]{2,1,0:T(8,128)(2,1)} custom-call(s32[4]{0:T(128)} %order.7, bf16[512,512]{1,0:T(8,128)(2,1)} %get-tuple-element.9.lown, bf16[4,512,128]{2,1,0:T(8,128)(2,1)} %get-tuple-element.10.lpiv, bf16[4,128,128]{2,1,0:T(8,128)(2,1)} %w_ref.5), custom_call_target="tpu_custom_call" | custom-call | tf_op jit(solution)/shard_map/combine/pallas_call | solution.py:253
  136.0 2.0 %all-to-all-done.4 = bf16[32,8,512]{2,1,0:T(8,128)(2,1)S(1)} async-done(((bf16[32,8,512]{2,1,0:T(8,128)(2,1)}), bf16[32,8,512]{2,1,0:T(8,128)(2,1)S(1)}, u32[]{:S(2)}, u32[]{:S(2)}) %all-to-all-start.4) | async-done | bytes 262176 | tf_op jit(solution)/shard_map/all_to_all | solution.py:250
  137.9 0.8 copy.18
  138.8 0.0 collective-permute-done.far
  138.8 10.9 %update.1 = bf16[4,128,32,128]{3,2,1,0:T(8,128)(2,1)} custom-call(s32[4]{0:T(128)} %order.7, s32[2]{0:T(128)} %pad_add_fusion.meta, s32[128]{0:T(128)} %reshape_reshape.3.mown, s32[128]{0:T(128)} %reshape.135.mpiv, bf16[4,128,32,128]{3,2,1,0:T(8,128)(2,1)} %bitcast.58, bf16[4,4,4,128,128]{4,3,2,1,0:T(8,128)(2,1)} %bitcast.55, ...), custom_call_target="tpu_custom_call" | custom-call | tf_op jit(solution)/shard_map/update/pallas_call | solution.py:262
  (28 shorter events, 0.1 us)
Async XLA Ops:
  3.2 2.8 %slice-start = ((bf16[4,1,128,256]{3,2,1,0:T(8,128)(2,1)}), bf16[1,1,128,256]{3,2,1,0:T(8,128)(2,1)S(1)}, s32[]{:S(2)}) async-start(bf16[4,1,128,256]{3,2,1,0:T(8,128)(2,1)} %param.8), calls=%async_computation.5 | async-start | bytes 131072 | tf_op jit(solution)/shard_map/slice | solution.py:196
  60.1 11.5 %copy-start = (bf16[16,512,128]{2,1,0:T(8,128)(2,1)}, bf16[16,512,128]{2,1,0:T(8,128)(2,1)S(1)}, u32[]{:S(2)}) copy-start(bf16[16,512,128]{2,1,0:T(8,128)(2,1)S(1)} %all_to_all.26) | copy-start | bytes 6291460
  60.1 78.6 %collective-permute-start = (bf16[4,4,4,128,128]{4,3,2,1,0:T(8,128)(2,1)S(1)}, bf16[4,4,4,128,128]{4,3,2,1,0:T(8,128)(2,1)}, u32[]{:S(2)}, u32[]{:S(2)}) collective-permute-start(bf16[4,4,4,128,128]{4,3,2,1,0:T(8,128)(2,1)S(1)} %bitcast.54), channel_id=1, source_target_pairs={{0,4},{4,0},{8,12},{12,8},{16,20},{20,16},{24,28},{28,24},{32,36},... | collective-permute-start | bytes 6291464 | tf_op jit(solution)/shard_map/ppermute | solution.py:209
  64.3 28.7 %all-to-all-start.1 = ((bf16[128,32,128]{2,1,0:T(8,128)(2,1)}), bf16[128,32,128]{2,1,0:T(8,128)(2,1)S(1)}, u32[]{:S(2)}, u32[]{:S(2)}) async-start(bf16[128,32,128]{2,1,0:T(8,128)(2,1)} %broadcast_in_dim.32), calls=%async_computation.1 | async-start | bytes 2097152 | tf_op jit(solution)/shard_map/all_to_all | solution.py:212
  71.5 19.6 %copy-start.7 = (bf16[8]{0:T(256)(128)(2,1)}, bf16[8]{0:T(256)(128)(2,1)S(1)}, u32[]{:S(2)}) copy-start(bf16[8]{0:T(256)(128)(2,1)S(1)} %pad_reduce_fusion) | copy-start | bytes 52
  71.7 25.4 %copy-start.2 = (bf16[520,128]{1,0:T(8,128)(2,1)}, bf16[520,128]{1,0:T(8,128)(2,1)S(1)}, u32[]{:S(2)}) copy-start(bf16[520,128]{1,0:T(8,128)(2,1)S(1)} %pad_maximum_fusion.1.own) | copy-start | bytes 399364
  71.7 13.9 %collective-permute-start.3 = (bf16[520,128]{1,0:T(8,128)(2,1)S(1)}, bf16[520,128]{1,0:T(8,128)(2,1)S(1)}, u32[]{:S(2)}, u32[]{:S(2)}) collective-permute-start(bf16[520,128]{1,0:T(8,128)(2,1)S(1)} %pad_maximum_fusion.1.own), channel_id=1, source_target_pairs={{0,3},{1,0},{2,1},{3,2},{4,7},{5,4},{6,5},{7,6},{8,11},{9,8},{10,9... | collective-permute-start | bytes 399368 | tf_op jit(solution)/shard_map/ppermute | solution.py:192
  74.4 12.8 %collective-permute-start.2 = (bf16[520,128]{1,0:T(8,128)(2,1)S(1)}, bf16[520,128]{1,0:T(8,128)(2,1)S(1)}, u32[]{:S(2)}, u32[]{:S(2)}) collective-permute-start(bf16[520,128]{1,0:T(8,128)(2,1)S(1)} %pad_maximum_fusion.1.own), channel_id=1, source_target_pairs={{0,2},{1,3},{2,0},{3,1},{4,6},{5,7},{6,4},{7,5},{8,10},{9,11},{10,... | collective-permute-start | bytes 399368 | tf_op jit(solution)/shard_map/ppermute | solution.py:192
  74.9 15.4 %collective-permute-start.1 = (bf16[520,128]{1,0:T(8,128)(2,1)S(1)}, bf16[520,128]{1,0:T(8,128)(2,1)}, u32[]{:S(2)}, u32[]{:S(2)}) collective-permute-start(bf16[520,128]{1,0:T(8,128)(2,1)S(1)} %pad_maximum_fusion.1.own), channel_id=1, source_target_pairs={{0,1},{1,2},{2,3},{3,0},{4,5},{5,6},{6,7},{7,4},{8,9},{9,10},{10,1... | collective-permute-start | bytes 399368 | tf_op jit(solution)/shard_map/ppermute | solution.py:192
  85.5 11.5 %copy-start.3 = (bf16[520,128]{1,0:T(8,128)(2,1)}, bf16[520,128]{1,0:T(8,128)(2,1)S(1)}, u32[]{:S(2)}) copy-start(bf16[520,128]{1,0:T(8,128)(2,1)S(1)} %collective-permute-done.3.d3) | copy-start | bytes 399364
  87.1 9.9 %copy-start.4 = (bf16[520,128]{1,0:T(8,128)(2,1)}, bf16[520,128]{1,0:T(8,128)(2,1)S(1)}, u32[]{:S(2)}) copy-start(bf16[520,128]{1,0:T(8,128)(2,1)S(1)} %collective-permute-done.2.d2) | copy-start | bytes 399364
  93.0 4.1 %copy-start.1 = (bf16[128,32,128]{2,1,0:T(8,128)(2,1)}, bf16[128,32,128]{2,1,0:T(8,128)(2,1)S(1)}, u32[]{:S(2)}) copy-start(bf16[128,32,128]{2,1,0:T(8,128)(2,1)S(1)} %all-to-all-done.1) | copy-start | bytes 3145732
  93.0 0.6 copy-start.5
  97.0 32.0 %copy-start.6 = (s32[4,32]{1,0:T(4,128)S(1)}, s32[4,32]{1,0:T(4,128)}, u32[]{:S(2)}) copy-start(s32[4,32]{1,0:T(4,128)} %get-tuple-element.22) | copy-start | bytes 1540
  125.3 12.6 %all-to-all-start.4 = ((bf16[32,8,512]{2,1,0:T(8,128)(2,1)}), bf16[32,8,512]{2,1,0:T(8,128)(2,1)S(1)}, u32[]{:S(2)}, u32[]{:S(2)}) async-start(bf16[32,8,512]{2,1,0:T(8,128)(2,1)} %solve.1), calls=%async_computation.4 | async-start | bytes 524288 | tf_op jit(solution)/shard_map/all_to_all | solution.py:250
